TPU v7x, 256 devices: a whole 4x4x8 slice. The times are simulated.
256 devices in a mesh: train: 16 (over y_lo, z), test: 16 (over x, y_hi, core).
Axes of the slice: x: 4, y: 4 (y_hi: 2, y_lo: 2; y = y_hi * 2 + y_lo), z: 8, core: 2. Of those that a mesh axis runs over, the one named last changes fastest.
Arguments:
- query_out: bfloat16 [4096, 3584], P('train', 'test'), may hold values from -16 to 16, as said below
- query_in: bfloat16 [4096, 3584], P('train', 'test'), may hold values from -6 to 6
- passage_out: bfloat16 [4096, 3584], P('train', 'test'), may hold values from -16 to 16, as said below
- passage_in_sum: bfloat16 [4096, 3584], P('train', 'test'), may hold values from -192 to 192
- passage_len: int32 [4096], P('train'), may hold values from 16 to 512
- positive: int32 [4096], P('train'), may hold values from 0 to 4095
- proj_in: bfloat16 [3584, 64], P('test'), may hold values from -0.09375 to 0.09375
- proj_out: bfloat16 [3584, 64], P('test'), may hold values from -0.09375 to 0.09375
- test_grads: bfloat16 [16384, 4096], P(('test', 'train')), may hold values from -6 to 6
Outputs:
- scores: float32 [4096, 16384], P('train', 'test')
Inputs may be any that keep to these rules, and one draw needn't show every extreme that they name: `query_out`: entries stay within the range. `passage_out`: entries stay within the range.
All inputs are finite; a program needn't handle non-finite values.
Results may differ from a plain program's by a relative error of at most 0.0034.
Values may be sent and summed in bfloat16 or wider, within the bound.
A program may use at most 64 MiB of HBM per device.

v0:
```python
import math

import jax
import jax.numpy as jnp
from jax import lax
from jax.sharding import PartitionSpec as P

D = 3584


def copy_for_each(value, axis):
    copies = jnp.broadcast_to(value, (lax.axis_size(axis), *value.shape))
    return lax.all_to_all(copies, axis, split_axis=0, concat_axis=0, tiled=True)


def laid_out(blocks, dim):
    dims = list(blocks.shape[1:])
    dims[dim] *= blocks.shape[0]
    return jnp.moveaxis(blocks, 0, dim).reshape(dims)


def gathered_copies(value, axis, dim):
    blocks = copy_for_each(value, axis)
    return laid_out(blocks, dim)


def taken_together(value, axis):
    return copy_for_each(value, axis).max(axis=0)


def over_copies(value, axis):
    everything = copy_for_each(value, axis)
    return jnp.sum(everything, axis=0)


def split_up(value, dim, count):
    dims = value.shape
    blocks = value.reshape(*dims[:dim], count, dims[dim] // count, *dims[dim + 1 :])
    return jnp.moveaxis(blocks, dim, 0)


def summed_on_arrival(value, axis, dim):
    count = lax.axis_size(axis)
    blocks = lax.all_to_all(split_up(value, dim, count), axis, 0, 0, tiled=True)
    return jnp.sum(blocks, axis=0)


def in_one(arrays, axis):
    ends = [0]
    for a in arrays:
        ends.append(ends[-1] + a.size)
    so_far = lax.psum(jnp.concatenate([a.ravel() for a in arrays]), axis)
    return tuple((so_far[b:e].reshape(a.shape) for a, b, e in zip(arrays, ends, ends[1:])))


def local(
    query_out,
    query_in,
    passage_out,
    passage_in_sum,
    passage_len,
    positive,
    proj_in,
    proj_out,
    test_grads,
):
    rank_size = proj_in.shape[1]
    logit_scale = 1.0 / math.sqrt(D)
    whole_pass = gathered_copies(passage_out, "train", 0)
    pass_block = lax.all_to_all(whole_pass, "test", split_axis=0, concat_axis=1, tiled=True)
    query_full = lax.all_gather(query_out, "test", axis=1, tiled=True)
    proj_full = gathered_copies(proj_out, "test", 0).astype(jnp.float32)
    block_logits = (
        lax.dot_general(
            query_full, pass_block, (((1,), (1,)), ((), ())), preferred_element_type=jnp.float32
        )
        * logit_scale
    )
    block_cols = block_logits.shape[1]
    block_top = taken_together(jnp.max(block_logits, axis=1), "test")
    block_exp = jnp.exp(block_logits - block_top[:, None])
    block_sum = over_copies(jnp.sum(block_exp, axis=1), "test")
    first_col = lax.axis_index("test") * block_cols
    col_index = lax.broadcasted_iota(jnp.int32, block_logits.shape, 1) + first_col
    block_hit = (col_index == positive[:, None]).astype(jnp.float32)
    block_grad = (block_exp / block_sum[:, None] - block_hit).astype(jnp.bfloat16)
    query_partial = (
        jnp.dot(block_grad, pass_block, preferred_element_type=jnp.float32) * logit_scale
    )
    out_query = jnp.dot(query_partial, proj_full, precision=lax.Precision.HIGHEST)
    pass_partial = (
        lax.dot_general(
            block_grad, query_full, (((0,), (0,)), ((), ())), preferred_element_type=jnp.float32
        )
        * logit_scale
    )
    pass_small = jnp.dot(pass_partial, proj_full, precision=lax.Precision.HIGHEST)
    padded = jnp.zeros((whole_pass.shape[0], rank_size), jnp.float32)
    padded = lax.dynamic_update_slice_in_dim(padded, pass_small, first_col, 0)
    out_pass = summed_on_arrival(padded, "train", 0)
    act_query = jnp.dot(query_in, proj_in, preferred_element_type=jnp.float32)
    act_pass = jnp.dot(passage_in_sum, proj_in, preferred_element_type=jnp.float32)
    act_query, act_pass, out_query, out_pass = in_one(
        (act_query, act_pass, out_query, out_pass), "test"
    )
    act_pass = act_pass / passage_len[:, None].astype(jnp.float32)
    stacked = jnp.stack((act_query, act_pass, out_query, out_pass), axis=1)
    row_count = stacked.shape[0]
    outer = (
        stacked[:, 0, :, None] * stacked[:, 2, None, :]
        + stacked[:, 1, :, None] * stacked[:, 3, None, :]
    )
    train_grads = outer.reshape(row_count, rank_size * rank_size).astype(jnp.bfloat16)
    return lax.dot_general(
        train_grads,
        lax.all_gather(test_grads, "train", axis=0, tiled=True),
        (((1,), (1,)), ((), ())),
        preferred_element_type=jnp.float32,
    )


def solution(mesh):
    return jax.shard_map(
        local,
        mesh=mesh,
        in_specs=(
            P("train", "test"),
            P("train", "test"),
            P("train", "test"),
            P("train", "test"),
            P("train"),
            P("train"),
            P("test", None),
            P("test", None),
            P(("test", "train"), None),
        ),
        out_specs=P("train", "test"),
        check_vma=False,
    )
```

profile of v0, /device:TPU:1, one launch (start us, length us, event | category | flops | bytes accessed | tf_op | source)
XLA Modules:
  0.0 403.7 jit_solution(1863392339717188709)
XLA Ops:
  7.4 2.4 broadcast_in_dim.19
  9.7 10.2 %all-to-all-start = ((bf16[16,256,224]{1,2,0:T(8,128)(2,1)}), bf16[16,256,224]{1,2,0:T(8,128)(2,1)}, u32[]{:S(2)}, u32[]{:S(2)}) async-start(bf16[16,256,224]{1,2,0:T(8,128)(2,1)} %broadcast_in_dim.19), calls=%async_computation | async-start | bytes 3670016 | tf_op jit(solution)/shard_map/all_to_all | solution.py:13
  20.0 0.7 all-gather.3.cloned.1.call-update
  20.7 41.4 %all-to-all-done = bf16[16,256,224]{1,2,0:T(8,128)(2,1)} async-done(((bf16[16,256,224]{1,2,0:T(8,128)(2,1)}), bf16[16,256,224]{1,2,0:T(8,128)(2,1)}, u32[]{:S(2)}, u32[]{:S(2)}) %all-to-all-start) | async-done | bytes 1835040 | tf_op jit(solution)/shard_map/all_to_all | solution.py:13
  62.0 9.3 %all-to-all-start.1 = ((bf16[16,256,224]{1,2,0:T(8,128)(2,1)}), bf16[16,256,224]{1,2,0:T(8,128)(2,1)S(1)}, u32[]{:S(2)}, u32[]{:S(2)}) async-start(bf16[16,256,224]{1,2,0:T(8,128)(2,1)} %all-to-all-done), calls=%async_computation.1 | async-start | bytes 3670016 | tf_op jit(solution)/shard_map/all_to_all | solution.py:70
  71.3 7.7 %all-gather.3.cloned.1.call-done = bf16[256,3584]{0,1:T(8,128)(2,1)} async-done(((bf16[256,224]{0,1:T(8,128)(2,1)}), bf16[256,3584]{0,1:T(8,128)(2,1)}) %all-gather.3.cloned.1.call-update) | async-done | bytes 1835024 | tf_op jit(solution)/shard_map/all_gather | solution.py:71
  79.0 17.8 %all-to-all-done.1 = bf16[16,256,224]{1,2,0:T(8,128)(2,1)S(1)} async-done(((bf16[16,256,224]{1,2,0:T(8,128)(2,1)}), bf16[16,256,224]{1,2,0:T(8,128)(2,1)S(1)}, u32[]{:S(2)}, u32[]{:S(2)}) %all-to-all-start.1) | async-done | bytes 1835040 | tf_op jit(solution)/shard_map/all_to_all | solution.py:70
  96.9 2.4 fusion.2
  99.2 13.2 %all_to_all.43 = f32[16,1,256]{2,1,0:T(1,128)S(1)} all-to-all(f32[16,1,256]{2,1,0:T(1,128)S(1)} %broadcast_in_dim.20), channel_id=1, replica_groups=mesh['train'=16,'test'=16] {'test'}, dimensions={0} | all-to-all | bytes 32768 | tf_op jit(solution)/shard_map/all_to_all | solution.py:13
  112.4 0.8 broadcast_in_dim.22
  113.3 3.8 all-to-all-start.4
  117.1 0.1 fusion
  117.2 11.1 %all-to-all-done.4 = bf16[16,224,64]{1,2,0:T(8,128)(2,1)S(1)} async-done(((bf16[16,224,64]{1,2,0:T(8,128)(2,1)}), bf16[16,224,64]{1,2,0:T(8,128)(2,1)S(1)}, u32[]{:S(2)}, u32[]{:S(2)}) %all-to-all-start.4) | async-done | bytes 458784 | tf_op jit(solution)/shard_map/all_to_all | solution.py:13
  128.3 0.6 broadcast_in_dim.21
  128.9 4.5 %all-to-all-start.3 = ((f32[16,1,256]{2,1,0:T(1,128)}), f32[16,1,256]{2,1,0:T(1,128)S(1)}, u32[]{:S(2)}, u32[]{:S(2)}) async-start(f32[16,1,256]{2,1,0:T(1,128)} %broadcast_in_dim.21), calls=%async_computation.3 | async-start | bytes 32768 | tf_op jit(solution)/shard_map/all_to_all | solution.py:13
  133.4 1.1 copy.55
  134.5 1.9 reshape.84
  136.4 4.4 %all-to-all-done.3 = f32[16,1,256]{2,1,0:T(1,128)S(1)} async-done(((f32[16,1,256]{2,1,0:T(1,128)}), f32[16,1,256]{2,1,0:T(1,128)S(1)}, u32[]{:S(2)}, u32[]{:S(2)}) %all-to-all-start.3) | async-done | bytes 16416 | tf_op jit(solution)/shard_map/all_to_all | solution.py:13
  140.8 2.2 convolution_multiply_fusion
  143.1 2.0 convolution_dynamic-update-slice_fusion
  145.1 1.1 copy.72
  146.2 4.8 %all-to-all-start.5 = ((f32[16,256,64]{1,2,0:T(8,128)}), f32[16,256,64]{1,2,0:T(8,128)S(1)}, u32[]{:S(2)}, u32[]{:S(2)}) async-start(f32[16,256,64]{1,2,0:T(8,128)} %bitcast.26), calls=%async_computation.5 | async-start | bytes 2097152 | tf_op jit(solution)/shard_map/all_to_all | solution.py:44
  151.1 0.9 fusion.3
  152.0 1.0 reshape.82
  153.0 1.8 fusion.4
  154.7 1.6 reshape.83
  156.3 1.8 convolution_multiply_fusion.1
  158.1 1.8 fusion.5
  159.9 0.1 reshape.85
  160.0 16.6 %all-to-all-done.5 = f32[16,256,64]{1,2,0:T(8,128)S(1)} async-done(((f32[16,256,64]{1,2,0:T(8,128)}), f32[16,256,64]{1,2,0:T(8,128)S(1)}, u32[]{:S(2)}, u32[]{:S(2)}) %all-to-all-start.5) | async-done | bytes 1048608 | tf_op jit(solution)/shard_map/all_to_all | solution.py:44
  176.7 0.1 copy.59
  176.8 0.1 reshape.87
  176.9 0.7 pad_maximum_fusion
  177.6 0.2 all-gather.5.cloned.1.call-start
  177.8 0.3 all-gather.5.cloned.1.call-update
  178.2 208.8 %all-reduce.2.cloned.1.call-done = f32[65536]{0:T(1024)} async-done(((f32[65536]{0:T(1024)}), f32[65536]{0:T(1024)}) %all-reduce.2.cloned.1.call-update) | async-done | bytes 262160 | tf_op jit(solution)/shard_map/psum | solution.py:52
  387.0 1.0 fusion.1
  387.9 0.1 slice.57
  388.0 0.1 broadcast_divide_fusion
  388.1 0.1 copy.62
  388.2 0.1 slice.53
  388.3 0.1 copy.60
  388.4 0.1 slice.55
  388.5 0.1 copy.61
  388.5 0.1 slice.59
  388.6 0.1 copy.63
  388.7 0.7 add_convert_fusion
  389.5 6.7 %fusion.6 = f32[256,1024]{1,0:T(8,128)} fusion(bf16[256,4096]{0,1:T(8,128)(2,1)S(1)} %bitcast.28, bf16[1024,4096]{1,0:T(8,128)(2,1)} %all-gather.5.cloned.1.call-done), kind=kOutput, calls=%fused_computation.17 | convolution fusion | flops 2147483648 | bytes 11534336 | tf_op jit(solution)/shard_map/dot_general | solution.py:114
  (31 shorter events, 0.4 us)
Async XLA Ops:
  7.4 143.7 %copy-start = (bf16[256,224]{0,1:T(8,128)(2,1)S(1)}, bf16[256,224]{0,1:T(8,128)(2,1)}, u32[]{:S(2)}) copy-start(bf16[256,224]{0,1:T(8,128)(2,1)} %param.10) | copy-start | bytes 344068
  9.7 52.3 %all-to-all-start = ((bf16[16,256,224]{1,2,0:T(8,128)(2,1)}), bf16[16,256,224]{1,2,0:T(8,128)(2,1)}, u32[]{:S(2)}, u32[]{:S(2)}) async-start(bf16[16,256,224]{1,2,0:T(8,128)(2,1)} %broadcast_in_dim.19), calls=%async_computation | async-start | bytes 3670016 | tf_op jit(solution)/shard_map/all_to_all | solution.py:13
  19.9 59.1 %all-gather.3.cloned.1.call-start = ((), (), s32[]{:S(2)}) async-start(), calls=%async_computation.6 | async-start | bytes 1949696 | tf_op jit(solution)/shard_map/all_gather | solution.py:71
  20.6 91.8 %copy-start.4 = (bf16[224,64]{0,1:T(8,128)(2,1)S(1)}, bf16[224,64]{0,1:T(8,128)(2,1)}, u32[]{:S(2)}) copy-start(bf16[224,64]{0,1:T(8,128)(2,1)} %param.16) | copy-start | bytes 86020
  62.0 34.8 %all-to-all-start.1 = ((bf16[16,256,224]{1,2,0:T(8,128)(2,1)}), bf16[16,256,224]{1,2,0:T(8,128)(2,1)S(1)}, u32[]{:S(2)}, u32[]{:S(2)}) async-start(bf16[16,256,224]{1,2,0:T(8,128)(2,1)} %all-to-all-done), calls=%async_computation.1 | async-start | bytes 3670016 | tf_op jit(solution)/shard_map/all_to_all | solution.py:70
  96.9 44.0 %copy-start.7 = (s32[256]{0:T(256)S(1)}, s32[256]{0:T(256)}, u32[]{:S(2)}) copy-start(s32[256]{0:T(256)} %param.14) | copy-start | bytes 3076
  99.2 43.8 %copy-start.1 = (f32[256,256]{0,1:T(8,128)}, f32[256,256]{0,1:T(8,128)S(1)}, u32[]{:S(2)}) copy-start(f32[256,256]{0,1:T(8,128)S(1)} %get-tuple-element.10) | copy-start | bytes 786436
  113.3 15.0 %all-to-all-start.4 = ((bf16[16,224,64]{1,2,0:T(8,128)(2,1)}), bf16[16,224,64]{1,2,0:T(8,128)(2,1)S(1)}, u32[]{:S(2)}, u32[]{:S(2)}) async-start(bf16[16,224,64]{1,2,0:T(8,128)(2,1)} %broadcast_in_dim.22), calls=%async_computation.4 | async-start | bytes 1048576 | tf_op jit(solution)/shard_map/all_to_all | solution.py:13
  117.1 26.0 %copy-start.5 = (f32[256]{0:T(256)}, f32[256]{0:T(256)S(1)}, u32[]{:S(2)}) copy-start(f32[256]{0:T(256)S(1)} %reduce_max.19) | copy-start | bytes 3076
  128.9 11.9 %all-to-all-start.3 = ((f32[16,1,256]{2,1,0:T(1,128)}), f32[16,1,256]{2,1,0:T(1,128)S(1)}, u32[]{:S(2)}, u32[]{:S(2)}) async-start(f32[16,1,256]{2,1,0:T(1,128)} %broadcast_in_dim.21), calls=%async_computation.3 | async-start | bytes 32768 | tf_op jit(solution)/shard_map/all_to_all | solution.py:13
  133.4 9.6 %copy-start.8 = (s32[256]{0:T(256)}, s32[256]{0:T(256)S(1)}, u32[]{:S(2)}) copy-start(s32[256]{0:T(256)S(1)} %iota_add_fusion) | copy-start | bytes 3076
  140.8 4.3 %copy-start.6 = (f32[256]{0:T(256)}, f32[256]{0:T(256)S(1)}, u32[]{:S(2)}) copy-start(f32[256]{0:T(256)S(1)} %reduce_sum.28) | copy-start | bytes 3076
  143.1 7.9 %copy-start.3 = (bf16[224,64]{0,1:T(8,128)(2,1)S(1)}, bf16[224,64]{0,1:T(8,128)(2,1)}, u32[]{:S(2)}) copy-start(bf16[224,64]{0,1:T(8,128)(2,1)} %param.15) | copy-start | bytes 86020
  146.2 30.4 %all-to-all-start.5 = ((f32[16,256,64]{1,2,0:T(8,128)}), f32[16,256,64]{1,2,0:T(8,128)S(1)}, u32[]{:S(2)}, u32[]{:S(2)}) async-start(f32[16,256,64]{1,2,0:T(8,128)} %bitcast.26), calls=%async_computation.5 | async-start | bytes 2097152 | tf_op jit(solution)/shard_map/all_to_all | solution.py:44
  151.0 235.9 %all-reduce.2.cloned.1.call-start = ((), (), s32[]{:S(2)}) async-start(), calls=%async_computation.7 | async-start | bytes 524288 | tf_op jit(solution)/shard_map/psum | solution.py:52
  158.1 18.7 %copy-start.2 = (f32[16384]{0:T(1024)S(1)}, f32[16384]{0:T(1024)}, u32[]{:S(2)}) copy-start(f32[16384]{0:T(1024)} %reshape.83) | copy-start | bytes 196612
  158.1 20.1 %copy-start.9 = (s32[256]{0:T(256)S(1)}, s32[256]{0:T(256)}, u32[]{:S(2)}) copy-start(s32[256]{0:T(256)} %param.13) | copy-start | bytes 3076
  177.6 211.9 %all-gather.5.cloned.1.call-start = ((), (), s32[]{:S(2)}) async-start(), calls=%async_computation.8 | async-start | bytes 8912896 | tf_op jit(solution)/shard_map/all_gather | solution.py:116
Sparse Core Ops, SparseCore 0:
  23.4 55.5 all-gather.2
  177.7 209.1 all-reduce.1
Sparse Core Ops, SparseCore 1:
  179.9 97.2 all-gather.4
where the time goes:
time: 404 us
  waiting for transfers between devices  309 us (76%)
  starting transfers between devices  32.9 us (8%)
  matrix products  19.4 us (5%)
  between operations  15.2 us (4%)
  blocking collectives  13.2 us (3%)
  local copies, waits for them, and re-layouts  12.5 us (3%)
    psum x1, waiting for transfers between devices, in_one(): so_far = lax.psum(jnp.concatenate([a.ravel() for a in arrays]), axis)  209 us
    all_to_all x3, waiting for transfers between devices, copy_for_each(): return lax.all_to_all(copies, axis, split_axis=0, concat_axis=0, tiled=True)  56.9 us
    all_to_all x3, starting transfers between devices, copy_for_each(): return lax.all_to_all(copies, axis, split_axis=0, concat_axis=0, tiled=True)  18.4 us
    all_to_all x1, waiting for transfers between devices, local(): lax.all_to_all(whole_pass, 'test', split_axis=0, concat_axis=1, tiled=True)  17.8 us
    all_to_all x1, waiting for transfers between devices, summed_on_arrival(): blocks = lax.all_to_all(split_up(value, dim, count), axis, 0, 0, tiled=True)  16.6 us
    all_to_all x1, blocking collectives, copy_for_each(): return lax.all_to_all(copies, axis, split_axis=0, concat_axis=0, tiled=True)  13.2 us
    all_to_all x1, starting transfers between devices, local(): lax.all_to_all(whole_pass, 'test', split_axis=0, concat_axis=1, tiled=True)  9.32 us
  transfers between devices with their start and end apart: 8, of which 7 were waited for; matrix products, arithmetic and copies ran while one was open for 4% of the time, Pallas kernels for 0%

commit v1 on v0

v1 whole, which is shorter than its diff:
```python
import math

import jax
import jax.numpy as jnp
from jax import lax
from jax.experimental import pallas as pl
from jax.experimental.pallas import tpu as pltpu
from jax.sharding import PartitionSpec as P

D = 3584
MESH = pl.DeviceIdType.MESH
F32, BF16 = jnp.float32, jnp.bfloat16

NAMES = {}


def sem_names():
    at = 0
    for name, count in (
        ("q1", 1), ("q10", 1), ("q2", 1), ("q3", 1), ("rq", 16),
        ("p", 1), ("p0", 1), ("rp", 1), ("pos", 1), ("rpos", 1),
        ("r1", 1), ("r10", 1), ("rr1", 1),
        ("pa", 4), ("pb", 3), ("ps", 1), ("rpa", 4), ("rpb", 3), ("rps", 1),
        ("lg", 1), ("ga", 4), ("gb", 3), ("rga", 4), ("rgb", 3),
        ("fa", 1), ("rfa", 1), ("qp", 1), ("rqp", 1), ("pp", 1), ("rpp", 1),
        ("st", 1), ("rst", 1), ("oq", 1), ("roq", 1), ("op", 1), ("rop", 1),
        ("fo", 1), ("rfo", 1), ("out", 2), ("rout", 2),
    ):
        NAMES[name] = at
        at += count
    return at


NSEM = sem_names()


def dev(x, y, z, c):
    return {"train": lax.rem(y, 2) * 8 + z, "test": x * 4 + lax.div(y, 2) * 2 + c}


def loop(first, last, body):
    def step(k, carry):
        body(k)
        return carry

    lax.fori_loop(first, last, step, 0)


def split(value):
    high = value.astype(BF16)
    return high, (value - high.astype(F32)).astype(BF16)


def kernel(
    q_ref, p_ref, qin_ref, pin_ref, len_ref, pos_ref, pjin_ref, pjout_ref, g_ref, out_ref,
    qj, pj, gb, r1s, r1r, fa, fo, qp2, pp2, st, oqs, oqr, ops, opr, posr, fat, fot, tt, outs, outr, sems,
):
    me_t, me_s = lax.axis_index("train"), lax.axis_index("test")
    b, z = lax.div(me_t, 8), lax.rem(me_t, 8)
    x, yh, c = lax.div(me_s, 4), lax.rem(lax.div(me_s, 2), 2), lax.rem(me_s, 2)
    y = yh * 2 + b
    q = x * 4 + y
    d = 1 - 2 * c
    scale = 1.0 / math.sqrt(D)

    def sem(name, k=0):
        return sems.at[NAMES[name] + k]

    def send(src, dst, ssem, rsem, to):
        pltpu.make_async_remote_copy(
            src_ref=src, dst_ref=dst, send_sem=ssem, recv_sem=rsem, device_id=to, device_id_type=MESH
        ).start()

    def wait(view, s):
        pltpu.make_async_copy(view, view, s).wait()

    def at_chip(k, core):
        q2 = lax.rem(q + k, 16)
        return q2, dev(lax.div(q2, 4), lax.rem(q2, 4), z, core)

    def near(src, dst, ssem, rsem):
        @pl.when(c == b)
        def _():
            pltpu.make_async_copy(src, dst, rsem).start()

        @pl.when(c != b)
        def _():
            send(src, dst, ssem, rsem, dev(x, y, z, b))

    barrier = pltpu.get_barrier_semaphore()

    def greet_plane(k):
        n = lax.rem(q * 2 + c + k, 32)
        q2 = lax.div(n, 2)
        pl.semaphore_signal(
            barrier, inc=1, device_id=dev(lax.div(q2, 4), lax.rem(q2, 4), z, lax.rem(n, 2)), device_id_type=MESH
        )

    def greet_ring(k):
        for core in range(2):
            pl.semaphore_signal(
                barrier, inc=1, device_id=dev(x, y, lax.rem(z + k, 8), core), device_id_type=MESH
            )

    loop(1, 32, greet_plane)
    loop(1, 8, greet_ring)
    pl.semaphore_wait(barrier, 45)

    slab = pl.ds(pl.multiple_of(z * 32 + b * 16, 16), 16)

    def send_p(k):
        q2, to = at_chip(k, b)
        send(p_ref.at[pl.ds(pl.multiple_of(q2 * 16, 16), 16)], pj.at[me_s, slab], sem("p"), sem("rp"), to)

    loop(1, 16, send_p)
    near(p_ref.at[pl.ds(pl.multiple_of(q * 16, 16), 16)], pj.at[me_s, slab], sem("p0"), sem("rp"))
    for k in (1, 3, 2):
        to = dev(lax.rem(x + k * c, 4), lax.rem(y + k * (1 - c), 4), z, b)
        send(q_ref, qj.at[me_s], sem("q1"), sem("rq", me_s), to)
    near(q_ref, qj.at[me_s], sem("q10"), sem("rq", me_s))
    send(pos_ref, posr, sem("pos"), sem("rpos"), dev(x, y + 1 - 2 * b, z, c))

    part = jnp.concatenate(
        [
            jnp.dot(pjin_ref[...], qin_ref[...], preferred_element_type=F32),
            jnp.dot(pjin_ref[...], pin_ref[...], preferred_element_type=F32) / len_ref[...].astype(F32),
            jnp.dot(pjout_ref[...], q_ref[...], preferred_element_type=F32),
            lax.dot_general(pjout_ref[...], p_ref[...], (((1,), (1,)), ((), ())), preferred_element_type=F32),
        ],
        axis=0,
    )
    r1s[...] = part.T.reshape(r1s.shape)

    def send_r1(k):
        q2, to = at_chip(k, b)
        send(r1s.at[q2], r1r.at[me_s], sem("r1"), sem("rr1"), to)

    loop(1, 16, send_r1)
    near(r1s.at[q], r1r.at[me_s], sem("r10"), sem("rr1"))

    to_a = dev(x, y, lax.rem(z + 8 + d, 8), c)
    to_b = dev(x, y, lax.rem(z + 8 - d, 8), c)
    to_sib = dev(x, y, z, 1 - c)

    def from_a(s):
        return lax.rem(z + 8 - d * s, 8)

    def from_b(s):
        return lax.rem(z + 8 + d * s, 8)

    def p_slab(zz):
        return pj.at[:, pl.ds(pl.multiple_of(zz * 32 + c * 16, 16), 16)]

    mine = p_slab(z)
    wait(mine, sem("rp"))
    send(mine, mine, sem("pa"), sem("rpa"), to_a)
    send(mine, mine, sem("pb"), sem("rpb"), to_b)
    send(mine, mine, sem("ps"), sem("rps"), to_sib)

    def start_g():
        pltpu.make_async_copy(g_ref, gb.at[z], sem("lg")).start()
        send(g_ref, gb.at[z], sem("ga"), sem("rga"), to_a)
        send(g_ref, gb.at[z], sem("gb"), sem("rgb"), to_b)

    def p_step(s):
        got = p_slab(from_a(s))
        wait(got, sem("rpa", s - 1))
        if s < 4:
            send(got, got, sem("pa", s), sem("rpa", s), to_a)
        send(got, got, sem("ps"), sem("rps"), to_sib)
        if s < 4:
            got = p_slab(from_b(s))
            wait(got, sem("rpb", s - 1))
            if s < 3:
                send(got, got, sem("pb", s), sem("rpb", s), to_b)
            send(got, got, sem("ps"), sem("rps"), to_sib)

    def g_step(s):
        got = gb.at[from_a(s)]
        wait(got, sem("rga", s - 1))
        if s < 4:
            send(got, got, sem("ga", s), sem("rga", s), to_a)
        if s < 4:
            got = gb.at[from_b(s)]
            wait(got, sem("rgb", s - 1))
            if s < 3:
                send(got, got, sem("gb", s), sem("rgb", s), to_b)

    start_g()

    for half in range(2):
        slot = x * 4 + half * 2
        wait(qj.at[slot], sem("rq", slot))
        for k in (1, 3, 2):
            send(qj.at[slot], qj.at[slot], sem("q2"), sem("rq", slot), dev(lax.rem(x + k, 4), y, z, c))

    @pl.when(c == b)
    def _():
        for x0 in range(4):
            slot = x0 * 4 + yh * 2 + 1
            wait(qj.at[slot], sem("rq", slot))
            for k in (1, 3, 2):
                send(qj.at[slot], qj.at[slot], sem("q3"), sem("rq", slot), dev(x, lax.rem(y + k, 4), z, c))

    p_step(1)

    wait(r1r, sem("rr1"))
    sums = jnp.sum(r1r[...], axis=0)
    row = c * 16 + q
    col = z * 2 + c
    fa[row] = sums[:, :128]
    qp2[q] = sums[:, 128:]
    pp2[col] = sums[:, 128:]

    def to_plane(buf, s, r):
        def body(k):
            n = lax.rem(q * 2 + c + k, 32)
            q2 = lax.div(n, 2)
            send(buf.at[row], buf.at[row], sem(s), sem(r), dev(lax.div(q2, 4), lax.rem(q2, 4), z, lax.rem(n, 2)))

        loop(1, 32, body)

    def to_column(src_of, dst, s, r):
        def body(k):
            n = lax.rem(col + k, 16)
            send(src_of(n), dst.at[col], sem(s), sem(r), dev(x, y, lax.div(n, 2), lax.rem(n, 2)))

        loop(1, 16, body)

    def to_chips(src_of, dst, s, r):
        def body(k):
            q2, to = at_chip(k, c)
            send(src_of(q2), dst.at[q], sem(s), sem(r), to)

        loop(1, 16, body)

    to_chips(lambda n: qp2.at[q], qp2, "qp", "rqp")
    to_column(lambda n: pp2.at[col], pp2, "pp", "rpp")
    to_plane(fa, "fa", "rfa")

    p_step(2)
    p_step(3)
    p_step(4)
    g_step(1)

    wait(pj.at[:, pl.ds(0, 128)], sem("rps"))
    for x0 in range(1, 4):
        for half in range(2):
            slot = lax.rem(x + x0, 4) * 4 + half * 2
            wait(qj.at[slot], sem("rq", slot))
    for x0 in range(4):
        for half in range(2):

            @pl.when(jnp.logical_or(c != b, yh != half))
            def _():
                slot = x0 * 4 + half * 2 + 1
                wait(qj.at[slot], sem("rq", slot))

    logits = jnp.dot(pj[0], qj[0], preferred_element_type=F32)
    for j in range(1, 16):
        logits += jnp.dot(pj[j], qj[j], preferred_element_type=F32)
    logits *= scale
    top = jnp.max(logits, axis=0, keepdims=True)
    total = jnp.sum(jnp.exp(logits - top), axis=0, keepdims=True)
    st[q, 0:1] = top
    st[q, 1:2] = total
    to_chips(lambda n: st.at[q], st, "st", "rst")
    wait(posr, sem("rpos"))
    positive = jnp.where(c == b, pos_ref[...], posr[...])
    at = lax.broadcasted_iota(jnp.int32, logits.shape, 0)
    passage = (((at >> 4) & 1) * 8 + (at >> 5)) * 256 + q * 16 + (at & 15)
    hit = (passage == positive).astype(F32)
    wait(qp2.at[pl.ds(0, 15)], sem("rqp"))
    wait(pp2.at[pl.ds(0, 15)], sem("rpp"))
    qp_high, qp_low = split(qp2[...].reshape(256, 128))
    pp_high, pp_low = split(pp2[...].reshape(256, 128).T)
    g_step(2)
    wait(st.at[pl.ds(0, 15)], sem("rst"))
    tops, totals = st[:, 0, :], st[:, 1, :]
    row_top = jnp.max(tops, axis=0, keepdims=True)
    row_sum = jnp.sum(totals * jnp.exp(tops - row_top), axis=0, keepdims=True)
    dlogit = (jnp.exp(logits - row_top) / row_sum - hit).astype(BF16)
    oq = jnp.dot(pp_high, dlogit, preferred_element_type=F32) + jnp.dot(pp_low, dlogit, preferred_element_type=F32)
    oqs[...] = (oq * scale).T.reshape(oqs.shape)
    to_chips(lambda n: oqs.at[n], oqr, "oq", "roq")
    op = jnp.dot(dlogit, qp_high, preferred_element_type=F32) + jnp.dot(dlogit, qp_low, preferred_element_type=F32)
    ops[...] = (op * scale).reshape(ops.shape)
    to_column(lambda n: ops.at[n], opr, "op", "rop")
    oqr[q] = oqs[q]
    opr[col] = ops[col]
    wait(fa.at[pl.ds(0, 31)], sem("rfa"))
    for i in range(2):
        fat[i] = fa[i * 16 : i * 16 + 16].reshape(256, 128).T
    wait(oqr.at[pl.ds(0, 15)], sem("roq"))
    wait(opr.at[pl.ds(0, 15)], sem("rop"))
    lane = lax.broadcasted_iota(jnp.int32, (16, 128), 1)
    fo[row] = jnp.where(lane < 64, jnp.sum(opr[...], axis=0), jnp.sum(oqr[...], axis=0))
    to_plane(fo, "fo", "rfo")
    g_step(3)
    wait(fo.at[pl.ds(0, 31)], sem("rfo"))
    for i in range(2):
        fot[i] = fo[i * 16 : i * 16 + 16].reshape(256, 128).T

    def build(block):
        op_t, oq_t = fot[block, 0:64], fot[block, 64:128]

        def body(r, carry):
            aq = fat[block, pl.ds(r, 1)]
            ap = fat[block, pl.ds(64 + r, 1)]
            tt[pl.ds(pl.multiple_of(r * 64, 64), 64)] = (aq * oq_t + ap * op_t).astype(BF16)
            return carry

        lax.fori_loop(0, 64, body, 0, unroll=4)

    build(1 - b)
    wait(g_ref, sem("lg"))
    g_step(4)
    partner = dev(x, y + 1 - 2 * b, z, c)
    for h in range(2):
        half = gb[h * 4 : h * 4 + 4].reshape(256, 4096)
        outs[h] = jnp.dot(half, tt[...], preferred_element_type=F32).astype(BF16)
        send(outs.at[h], outr.at[h], sem("out", h), sem("rout", h), partner)
    build(b)
    for h in range(2):
        half = gb[h * 4 : h * 4 + 4].reshape(256, 4096)
        out_ref[b, h * 256 : h * 256 + 256] = jnp.dot(half, tt[...], preferred_element_type=F32)

    wait(p_ref.at[pl.ds(0, 240)], sem("p"))
    wait(qj.at[pl.ds(0, 3)], sem("q1"))
    wait(r1s.at[pl.ds(0, 15)], sem("r1"))
    wait(pos_ref, sem("pos"))
    wait(qj.at[pl.ds(0, 6)], sem("q2"))

    @pl.when(c == b)
    def _():
        wait(qj.at[pl.ds(0, 12)], sem("q3"))

    @pl.when(c != b)
    def _():
        wait(p_ref.at[pl.ds(0, 16)], sem("p0"))
        wait(qj.at[0], sem("q10"))
        wait(r1s.at[0], sem("r10"))

    for s in range(4):
        wait(mine, sem("pa", s))
        wait(g_ref, sem("ga", s))
    for s in range(3):
        wait(mine, sem("pb", s))
        wait(g_ref, sem("gb", s))
    wait(pj.at[:, pl.ds(0, 128)], sem("ps"))
    wait(qp2.at[pl.ds(0, 15)], sem("qp"))
    wait(pp2.at[pl.ds(0, 15)], sem("pp"))
    wait(fa.at[pl.ds(0, 31)], sem("fa"))
    wait(st.at[pl.ds(0, 15)], sem("st"))
    wait(oqs.at[pl.ds(0, 15)], sem("oq"))
    wait(ops.at[pl.ds(0, 15)], sem("op"))
    wait(fo.at[pl.ds(0, 31)], sem("fo"))
    for h in range(2):
        wait(outr.at[h], sem("rout", h))
        out_ref[1 - b, h * 256 : h * 256 + 256] = outr[h].astype(F32)
        wait(outs.at[h], sem("out", h))


def local(
    query_out, query_in, passage_out, passage_in_sum, passage_len, positive, proj_in, proj_out, test_grads
):
    vmem = pl.BlockSpec(memory_space=pltpu.VMEM)
    out = pl.pallas_call(
        kernel,
        name="attribution",
        out_shape=jax.ShapeDtypeStruct((2, 512, 256), F32),
        in_specs=[vmem] * 8 + [pl.BlockSpec(memory_space=pl.ANY)],
        out_specs=vmem,
        scratch_shapes=[
            pltpu.VMEM((16, 224, 256), BF16),
            pltpu.VMEM((16, 256, 224), BF16),
            pltpu.VMEM((8, 64, 4096), BF16),
            pltpu.VMEM((16, 16, 256), F32),
            pltpu.VMEM((16, 16, 256), F32),
            pltpu.VMEM((32, 16, 128), F32),
            pltpu.VMEM((32, 16, 128), F32),
            pltpu.VMEM((16, 16, 128), F32),
            pltpu.VMEM((16, 16, 128), F32),
            pltpu.VMEM((16, 2, 256), F32),
            pltpu.VMEM((16, 16, 128), F32),
            pltpu.VMEM((16, 16, 128), F32),
            pltpu.VMEM((16, 16, 128), F32),
            pltpu.VMEM((16, 16, 128), F32),
            pltpu.VMEM((1, 256), jnp.int32),
            pltpu.VMEM((2, 128, 256), F32),
            pltpu.VMEM((2, 128, 256), F32),
            pltpu.VMEM((4096, 256), BF16),
            pltpu.VMEM((2, 256, 256), BF16),
            pltpu.VMEM((2, 256, 256), BF16),
            pltpu.SemaphoreType.DMA((NSEM,)),
        ],
        compiler_params=pltpu.CompilerParams(
            collective_id=0, has_side_effects=True, vmem_limit_bytes=48 * 1024 * 1024
        ),
    )(
        query_out.T,
        passage_out,
        query_in.T,
        passage_in_sum.T,
        passage_len[None, :],
        positive[None, :],
        proj_in.T,
        proj_out.T,
        test_grads,
    )
    return out.reshape(1024, 256).T


def solution(mesh):
    return jax.shard_map(
        local,
        mesh=mesh,
        in_specs=(
            P("train", "test"),
            P("train", "test"),
            P("train", "test"),
            P("train", "test"),
            P("train"),
            P("train"),
            P("test", None),
            P("test", None),
            P(("test", "train"), None),
        ),
        out_specs=P("train", "test"),
        check_vma=False,
    )
```

time: 404 us -> 96.7 us (0.24)
  waiting for transfers between devices: 309 us -> 0 us
  Pallas kernels: 0 us -> 90.5 us
  starting transfers between devices: 32.9 us -> 0 us
  matrix products: 19.4 us -> 0 us
  between operations: 15.2 us -> 0.07 us
  blocking collectives: 13.2 us -> 0 us
  local copies, waits for them, and re-layouts: 12.5 us -> 5.81 us
    psum x1 -> x0, waiting for transfers between devices: 209 us -> none  [in_one(): so_far = lax.psum(jnp.concatenate([a.ravel() for a in arrays]), axis)]
    all_to_all x5 -> x0, waiting for transfers between devices: 91.3 us -> none  [the longest x3 56.9 us: copy_for_each(): return lax.all_to_all(copies, axis, split_axis=0, concat_axis=0, tiled=True)]
    pallas_call x0 -> x1, Pallas kernels: none -> 90.5 us  [local(): pl.pallas_call(kernel, name='attribution', out_shape=jax.ShapeDtypeStruct...]
    all_to_all x5 -> x0, starting transfers between devices: 32.6 us -> none  [the longest x3 18.4 us: copy_for_each(): return lax.all_to_all(copies, axis, split_axis=0, concat_axis=0, tiled=True)]
    dot_general x8 -> x0, matrix products: 19.4 us -> none  [the longest x1 6.74 us: local(): lax.dot_general(train_grads, lax.all_gather(test_grads, 'train', axis=0,...]
    all_to_all x1 -> x0, blocking collectives: 13.2 us -> none  [copy_for_each(): return lax.all_to_all(copies, axis, split_axis=0, concat_axis=0, tiled=True)]
    all_gather x2 -> x0, waiting for transfers between devices: 7.71 us -> none  [the longest x1 7.69 us: local(): query_full = lax.all_gather(query_out, 'test', axis=1, tiled=True)]
    unnamed x20 -> x17, local copies, waits for them, and re-layouts: 0.05 us -> 4.5 us
  transfers between devices with their start and end apart: 8 -> 0, of which waited for: 7 -> 0; matrix products, arithmetic and copies ran while one was open for 4% -> 0% of each run, Pallas kernels for 0% -> 0%
where the time goes in v1:
time: 96.7 us; the launch traced here: 96.4 us
  Pallas kernels  90.5 us (94%)
  local copies, waits for them, and re-layouts  5.81 us (6%)
    pallas_call x1, Pallas kernels, local(): pl.pallas_call(kernel, name='attribution', out_shape=jax.ShapeDtypeStruct...  90.5 us
    unnamed x17, local copies, waits for them, and re-layouts  4.5 us

profile of v1, /device:TPU:1, one launch (start us, length us, event | category | flops | bytes accessed | tf_op | source)
XLA Modules:
  0.0 96.4 jit_solution(1106286117859158380)
XLA Ops:
  0.0 0.0 copy-start.1
  0.0 0.0 copy-start.2
  0.0 0.0 copy-start.6
  0.0 0.0 copy-start.7
  0.0 1.0 %copy.10.p_ref = bf16[256,224]{1,0:T(8,128)(2,1)S(1)} copy(bf16[256,224]{0,1:T(8,128)(2,1)} %param.11) | data formatting | bytes 229376 | tf_op args[2]
  1.1 0.0 copy-done.1
  1.1 0.0 copy-done.2
  1.1 0.0 copy-done.6
  1.1 0.0 copy-done.7
  1.1 0.0 copy-start
  1.1 1.0 %copy-done = bf16[64,4096]{1,0:T(8,128)(2,1)S(1)} copy-done((bf16[64,4096]{1,0:T(8,128)(2,1)S(1)}, bf16[64,4096]{1,0:T(8,128)(2,1)}, u32[]{:S(2)}) %copy-start) | copy-done | bytes 524312
  2.1 0.0 copy-start.3
  2.1 0.9 copy-done.3
  3.0 0.0 copy-start.4
  3.0 0.8 copy-done.4
  3.8 0.0 copy-start.5
  3.8 0.8 copy-done.5
  4.6 90.5 %attribution.1 = f32[2,512,256]{2,1,0:T(8,128)S(1)} custom-call(bf16[224,256]{1,0:T(8,128)(2,1)S(1)} %bitcast.10, bf16[256,224]{1,0:T(8,128)(2,1)S(1)} %copy.10.p_ref, bf16[224,256]{1,0:T(8,128)(2,1)S(1)} %bitcast.11, bf16[224,256]{1,0:T(8,128)(2,1)S(1)} %bitcast.12, s32[1,256]{1,0:T(1,128)S(1)} %bitcast.15, s32[1,256]{1,0:T(1,128)S(1)} %bitcast.16, ...), custom_call_target="tpu_custom_call" | custom-call | tf_op jit(solution)/shard_map/attribution/pallas_call | solution.py:368
  95.0 1.3 %copy.11 = f32[1024,256]{0,1:T(8,128)} copy(f32[1024,256]{1,0:T(8,128)S(1)} %bitcast.9) | data formatting | bytes 2097152 | tf_op jit(solution)/shard_map/reshape | solution.py:411
Async XLA Ops:
  0.0 1.1 %copy-start.1 = (bf16[256,224]{0,1:T(8,128)(2,1)S(1)}, bf16[256,224]{0,1:T(8,128)(2,1)}, u32[]{:S(2)}) copy-start(bf16[256,224]{0,1:T(8,128)(2,1)} %param.9) | copy-start | bytes 344068
  0.0 1.1 %copy-start.2 = (bf16[256,224]{0,1:T(8,128)(2,1)S(1)}, bf16[256,224]{0,1:T(8,128)(2,1)}, u32[]{:S(2)}) copy-start(bf16[256,224]{0,1:T(8,128)(2,1)} %param.10) | copy-start | bytes 344068
  0.0 1.1 %copy-start.6 = (s32[256]{0:T(256)S(1)}, s32[256]{0:T(256)}, u32[]{:S(2)}) copy-start(s32[256]{0:T(256)} %param.13) | copy-start | bytes 3076
  0.0 1.1 %copy-start.7 = (s32[256]{0:T(256)S(1)}, s32[256]{0:T(256)}, u32[]{:S(2)}) copy-start(s32[256]{0:T(256)} %param.14) | copy-start | bytes 3076
  1.1 1.0 %copy-start = (bf16[64,4096]{1,0:T(8,128)(2,1)S(1)}, bf16[64,4096]{1,0:T(8,128)(2,1)}, u32[]{:S(2)}) copy-start(bf16[64,4096]{1,0:T(8,128)(2,1)} %g_ref.1) | copy-start | bytes 1572868
  2.1 0.9 copy-start.3
  3.0 0.8 copy-start.4
  3.8 0.8 copy-start.5

commit v2 on v1

v2 whole, which is shorter than its diff:
```python
import math

import jax
import jax.numpy as jnp
from jax import lax
from jax.experimental import pallas as pl
from jax.experimental.pallas import tpu as pltpu
from jax.sharding import PartitionSpec as P

D = 3584
MESH = pl.DeviceIdType.MESH
F32, BF16 = jnp.float32, jnp.bfloat16

NAMES = {}


def sem_names():
    at = 0
    for name, count in (
        ("in", 8), ("q1", 1), ("q10", 1), ("q2", 1), ("rq", 16),
        ("p", 1), ("p0", 1), ("rp", 1), ("pos", 1), ("rpos", 1),
        ("r1", 1), ("r10", 1), ("rr1", 1),
        ("pa", 1), ("pb", 1), ("ps", 1), ("rpa", 4), ("rpb", 3), ("rps", 1),
        ("lg", 1), ("ga", 1), ("gb", 1), ("rga", 16), ("rgb", 12),
        ("fa", 1), ("rfa", 1),
        ("st", 1), ("rst", 1), ("oq", 1), ("roq", 1), ("op", 1), ("rop", 1),
        ("fo", 1), ("rfo", 1), ("out", 2), ("rout", 2),
    ):
        NAMES[name] = at
        at += count
    return at


NSEM = sem_names()


def dev(x, y, z, c):
    return {"train": lax.rem(y, 2) * 8 + z, "test": x * 4 + lax.div(y, 2) * 2 + c}


def loop(first, last, body):
    def step(k, carry):
        body(k)
        return carry

    lax.fori_loop(first, last, step, 0)


def split(value):
    high = value.astype(BF16)
    return high, (value - high.astype(F32)).astype(BF16)


def dot(a, b, dims=((1,), (0,))):
    return lax.dot_general(a, b, (dims, ((), ())), preferred_element_type=F32)


def kernel(
    q_hbm, p_hbm, qin_hbm, pin_hbm, len_hbm, pos_hbm, pjin_hbm, pjout_hbm, g_ref, out_ref,
    qx, pt, pr, qin, pin, plen, posv, pjin, pjout,
    qj, pj, gb, r1s, r1r, fa, fo, st, oqs, oqr, ops, opr, posr, fat, fot, tt, outs, outr, sems,
):
    me_t, me_s = lax.axis_index("train"), lax.axis_index("test")
    b, z = lax.div(me_t, 8), lax.rem(me_t, 8)
    x, yh, c = lax.div(me_s, 4), lax.rem(lax.div(me_s, 2), 2), lax.rem(me_s, 2)
    y = yh * 2 + b
    q = x * 4 + y
    d = 1 - 2 * c
    row = c * 16 + q
    col = z * 2 + c
    scale = 1.0 / math.sqrt(D)

    def sem(name, k=0):
        return sems.at[NAMES[name] + k]

    def send(src, dst, ssem, rsem, to):
        pltpu.make_async_remote_copy(
            src_ref=src, dst_ref=dst, send_sem=ssem, recv_sem=rsem, device_id=to, device_id_type=MESH
        ).start()

    def wait(view, s):
        pltpu.make_async_copy(view, view, s).wait()

    def at_chip(k, core):
        q2 = lax.rem(q + k, 16)
        return q2, dev(lax.div(q2, 4), lax.rem(q2, 4), z, core)

    def beside(dx, dy, core):
        return dev(lax.rem(x + 4 + dx, 4), lax.rem(y + 4 + dy, 4), z, core)

    def near(src, dst, ssem, rsem):
        @pl.when(c == b)
        def _():
            pltpu.make_async_copy(src, dst, rsem).start()

        @pl.when(c != b)
        def _():
            send(src, dst, ssem, rsem, dev(x, y, z, b))

    loads = ((q_hbm, qx.at[0:224]), (p_hbm, pt), (qin_hbm, qin), (pin_hbm, pin), (len_hbm, plen), (pos_hbm, posv), (pjin_hbm, pjin), (pjout_hbm, pjout))
    loads = [pltpu.make_async_copy(a, v, sem("in", i)) for i, (a, v) in enumerate(loads)]
    for i in (1, 0, 7, 2, 3, 4, 6, 5):
        loads[i].start()
    pltpu.make_async_copy(g_ref, gb.at[0], sem("lg")).start()
    barrier = pltpu.get_barrier_semaphore()

    def greet_plane(k):
        n = lax.rem(q * 2 + c + k, 32)
        q2 = lax.div(n, 2)
        pl.semaphore_signal(
            barrier, inc=1, device_id=dev(lax.div(q2, 4), lax.rem(q2, 4), z, lax.rem(n, 2)), device_id_type=MESH
        )

    def greet_ring(k):
        for core in range(2):
            pl.semaphore_signal(
                barrier, inc=1, device_id=dev(x, y, lax.rem(z + k, 8), core), device_id_type=MESH
            )

    loop(1, 8, greet_ring)
    loop(1, 32, greet_plane)
    loads[1].wait()
    pr[...] = pt[...].T
    loads[7].wait()
    qx[224:288, 128:256] = jnp.zeros((64, 128), BF16)
    qx[224:288, 0:224] = pjout[...]
    for i in (0, 2, 3, 4, 6, 5):
        loads[i].wait()
    part = jnp.concatenate([dot(pjin[...], qin[...]), dot(pjin[...], pin[...]) / plen[...].astype(F32)], axis=0)
    r1s[...] = part.T.reshape(r1s.shape)
    pl.semaphore_wait(barrier, 45)

    slab = pl.ds(pl.multiple_of(z * 32 + b * 16, 16), 16)

    def send_p(k):
        q2, to = at_chip(k, b)
        send(pr.at[pl.ds(pl.multiple_of(q2 * 16, 16), 16)], pj.at[me_s, slab], sem("p"), sem("rp"), to)

    loop(1, 16, send_p)
    near(pr.at[pl.ds(pl.multiple_of(q * 16, 16), 16)], pj.at[me_s, slab], sem("p0"), sem("rp"))
    near(qx, qj.at[me_s], sem("q10"), sem("rq", me_s))
    for k in (1, -1):
        send(qx, qj.at[me_s], sem("q1"), sem("rq", me_s), beside(k * c, k * (1 - c), b))
    send(posv, posr, sem("pos"), sem("rpos"), dev(x, y + 1 - 2 * b, z, c))

    to_a = dev(x, y, lax.rem(z + 8 + d, 8), c)
    to_b = dev(x, y, lax.rem(z + 8 - d, 8), c)
    to_sib = dev(x, y, z, 1 - c)

    def from_a(s):
        return lax.rem(z + 8 - d * s, 8)

    def from_b(s):
        return lax.rem(z + 8 + d * s, 8)

    def p_slab(zz):
        return pj.at[:, pl.ds(pl.multiple_of(zz * 32 + c * 16, 16), 16)]

    def p_step(s):
        got = p_slab(from_a(s))
        wait(got, sem("rpa", s - 1))
        if s < 4:
            send(got, got, sem("pa"), sem("rpa", s), to_a)
        send(got, got, sem("ps"), sem("rps"), to_sib)
        if s < 4:
            got = p_slab(from_b(s))
            wait(got, sem("rpb", s - 1))
            if s < 3:
                send(got, got, sem("pb"), sem("rpb", s), to_b)
            send(got, got, sem("ps"), sem("rps"), to_sib)

    def g_event(e):
        s, rows = e // 4 + 1, slice(e % 4 * 16, e % 4 * 16 + 16)
        if e < 16:
            src = g_ref.at[rows]
            if s > 1:
                src = gb.at[2 * s - 3, rows]
                wait(src, sem("rga", e - 4))
            send(src, gb.at[2 * s - 1, rows], sem("ga"), sem("rga", e), to_a)
        if e < 12:
            src = g_ref.at[rows]
            if s > 1:
                src = gb.at[2 * s - 2, rows]
                wait(src, sem("rgb", e - 4))
            send(src, gb.at[2 * s, rows], sem("gb"), sem("rgb", e), to_b)

    g_event(0)
    g_event(1)

    def send_r1(k):
        q2, to = at_chip(k, b)
        send(r1s.at[q2], r1r.at[me_s], sem("r1"), sem("rr1"), to)

    loop(1, 16, send_r1)
    near(r1s.at[q], r1r.at[me_s], sem("r10"), sem("rr1"))

    HALVES = (slice(0, 144), slice(144, 288))

    def got_q(x0, half, core):
        slot = x0 * 4 + half * 2 + core
        wait(qj.at[slot], sem("rq", slot))
        return slot

    def pass_q(slot, dx, dy):
        send(qj.at[slot], qj.at[slot], sem("q2"), sem("rq", slot), beside(dx, dy, c))

    def pass_half(slot, h, dx, dy):
        view = qj.at[slot, HALVES[h]]
        send(view, view, sem("q2"), sem("rq", slot), beside(dx, dy, c))

    below, above = lax.div(lax.rem(y + 3, 4), 2), lax.div(lax.rem(y + 1, 4), 2)

    @pl.when(c == b)
    def _():
        slot = got_q(x, yh, 0)
        pass_q(slot, 1, 0)
        pass_q(slot, -1, 0)
        slot = got_q(x, yh, 1)
        pass_q(slot, 0, 1)
        pass_q(slot, 0, -1)

    mine = p_slab(z)
    wait(mine, sem("rp"))
    send(mine, mine, sem("pa"), sem("rpa"), to_a)
    send(mine, mine, sem("pb"), sem("rpb"), to_b)
    send(mine, mine, sem("ps"), sem("rps"), to_sib)

    @pl.when(c == b)
    def _():
        for h, dx in ((0, 1), (1, -1)):
            slot = got_q(lax.rem(x + 4 - dx, 4), yh, 1)
            pass_half(slot, h, dx, 0)
            pass_q(slot, 0, 1)
            pass_q(slot, 0, -1)

    @pl.when(c != b)
    def _():
        for h, dy, half in ((0, 1, below), (1, -1, above)):
            slot = got_q(x, half, 0)
            pass_half(slot, h, 0, dy)
            pass_q(slot, 1, 0)
            pass_q(slot, -1, 0)

    p_step(1)
    g_event(2)

    @pl.when(c == b)
    def _():
        slot = got_q(x, 1 - yh, 0)
        pass_q(slot, 1, 0)
        pass_q(slot, -1, 0)
        slot = got_q(lax.rem(x + 2, 4), yh, 1)
        pass_q(slot, 0, 1)
        pass_q(slot, 0, -1)

    @pl.when(c != b)
    def _():
        for x0 in (0, 1, 3):
            for h, dy, half in ((0, 1, below), (1, -1, above)):
                pass_half(got_q(lax.rem(x + x0, 4), half, 1), h, 0, dy)

    for h, dx in ((0, 1), (1, -1)):
        for half in range(2):
            pass_half(got_q(lax.rem(x + 4 - dx, 4), half, 0), h, dx, 0)

    p_step(2)
    g_event(3)

    @pl.when(c != b)
    def _():
        for h, dy, half in ((0, 1, below), (1, -1, above)):
            pass_half(got_q(lax.rem(x + 2, 4), half, 1), h, 0, dy)

    wait(r1r, sem("rr1"))
    fa[row] = jnp.sum(r1r[...], axis=0)
    p_step(3)
    g_event(4)
    p_step(4)
    g_event(5)

    def to_plane(buf, s, r):
        def body(k):
            n = lax.rem(q * 2 + c + k, 32)
            q2 = lax.div(n, 2)
            send(buf.at[row], buf.at[row], sem(s), sem(r), dev(lax.div(q2, 4), lax.rem(q2, 4), z, lax.rem(n, 2)))

        loop(1, 32, body)

    def to_column(src_of, dst, s, r):
        def body(k):
            n = lax.rem(col + k, 16)
            send(src_of(n), dst.at[col], sem(s), sem(r), dev(x, y, lax.div(n, 2), lax.rem(n, 2)))

        loop(1, 16, body)

    def to_chips(src_of, dst, s, r):
        def body(k):
            q2, to = at_chip(k, c)
            send(src_of(q2), dst.at[q], sem(s), sem(r), to)

        loop(1, 16, body)

    for half in range(2):
        got_q(lax.rem(x + 2, 4), half, 0)

    @pl.when(c == b)
    def _():
        for x0 in range(4):
            got_q(x0, 1 - yh, 1)

    wait(pj.at[:, pl.ds(0, 128)], sem("rps"))
    logits = dot(pj[0], qj[0, 0:224])
    for j in range(1, 16):
        logits += dot(pj[j], qj[j, 0:224])
    logits *= scale
    top = jnp.max(logits, axis=0, keepdims=True)
    total = jnp.sum(jnp.exp(logits - top), axis=0, keepdims=True)
    st[q, 0:1] = top
    st[q, 1:2] = total
    to_chips(lambda n: st.at[q], st, "st", "rst")
    to_plane(fa, "fa", "rfa")
    g_event(6)
    wait(posr, sem("rpos"))
    positive = jnp.where(c == b, posv[...], posr[...])
    at = lax.broadcasted_iota(jnp.int32, logits.shape, 0)
    passage = (((at >> 4) & 1) * 8 + (at >> 5)) * 256 + q * 16 + (at & 15)
    hit = (passage == positive).astype(F32)
    qp_t = dot(qj[0, 224:288, 0:224], qj[0, 0:224])
    pp_t = dot(qj[0, 224:288, 0:224], pj[0], ((1,), (1,)))
    for j in range(1, 16):
        qp_t += dot(qj[j, 224:288, 0:224], qj[j, 0:224])
        pp_t += dot(qj[j, 224:288, 0:224], pj[j], ((1,), (1,)))
    qp_high, qp_low = split(qp_t)
    pp_high, pp_low = split(pp_t)
    wait(st.at[pl.ds(0, 15)], sem("rst"))
    tops, totals = st[:, 0, :], st[:, 1, :]
    row_top = jnp.max(tops, axis=0, keepdims=True)
    row_sum = jnp.sum(totals * jnp.exp(tops - row_top), axis=0, keepdims=True)
    dlogit = (jnp.exp(logits - row_top) / row_sum - hit).astype(BF16)
    op = dot(dlogit, qp_high, ((1,), (1,))) + dot(dlogit, qp_low, ((1,), (1,)))
    ops[...] = (op * scale).reshape(ops.shape)
    to_column(lambda n: ops.at[n], opr, "op", "rop")
    oq = dot(pp_high, dlogit) + dot(pp_low, dlogit)
    oqs[...] = (oq * scale).T.reshape(oqs.shape)
    to_chips(lambda n: oqs.at[n], oqr, "oq", "roq")
    oqr[q] = oqs[q]
    opr[col] = ops[col]
    g_event(7)
    g_event(8)
    wait(fa.at[pl.ds(0, 31)], sem("rfa"))
    for i in range(2):
        fat[i] = fa[i * 16 : i * 16 + 16].reshape(256, 128).T
    wait(oqr.at[pl.ds(0, 15)], sem("roq"))
    wait(opr.at[pl.ds(0, 15)], sem("rop"))
    fo[row] = jnp.concatenate([jnp.sum(opr[...], axis=0), jnp.sum(oqr[...], axis=0)], axis=1)
    to_plane(fo, "fo", "rfo")
    g_event(9)
    g_event(10)
    g_event(11)
    wait(fo.at[pl.ds(0, 31)], sem("rfo"))
    for i in range(2):
        fot[i] = fo[i * 16 : i * 16 + 16].reshape(256, 128).T

    def build(n, block):
        op_t, oq_t = fot[block, 0:64], fot[block, 64:128]

        def body(r, carry):
            aq = fat[block, pl.ds(r, 1)]
            ap = fat[block, pl.ds(64 + r, 1)]
            tt[n, pl.ds(pl.multiple_of(r * 64, 64), 64)] = (aq * oq_t + ap * op_t).astype(BF16)
            return carry

        lax.fori_loop(0, 64, body, 0, unroll=4)

    def place(slot):
        if slot == 0:
            at = z
        elif slot % 2:
            at = from_a((slot + 1) // 2)
        else:
            at = from_b(slot // 2)
        return pl.ds(pl.multiple_of(at * 64, 64), 64)

    partner = dev(x, y + 1 - 2 * b, z, c)

    def product(n, h):
        return dot(gb[h * 4 : h * 4 + 4].reshape(256, 4096), tt[n])

    def swap(h):
        outs[h] = product(0, h).astype(BF16)
        send(outs.at[h], outr.at[h], sem("out", h), sem("rout", h), partner)

    def keep(h):
        mine = product(1, h)
        for i in range(4):
            out_ref[b, place(h * 4 + i)] = mine[i * 64 : i * 64 + 64]

    build(0, 1 - b)
    g_event(12)
    g_event(13)
    wait(gb.at[0], sem("lg"))
    swap(0)
    g_event(14)
    build(1, b)
    keep(0)
    g_event(15)
    for e in range(12, 16):
        wait(gb.at[7, e % 4 * 16 : e % 4 * 16 + 16], sem("rga", e))
    for e in range(8, 12):
        wait(gb.at[6, e % 4 * 16 : e % 4 * 16 + 16], sem("rgb", e))
    swap(1)
    keep(1)

    wait(pr.at[pl.ds(0, 240)], sem("p"))
    wait(qj.at[pl.ds(0, 2)], sem("q1"))
    wait(r1s.at[pl.ds(0, 15)], sem("r1"))
    wait(posv, sem("pos"))

    @pl.when(c == b)
    def _():
        wait(qj.at[pl.ds(0, 15)], sem("q2"))

    @pl.when(c != b)
    def _():
        wait(qj.at[pl.ds(0, 11)], sem("q2"))
        wait(pr.at[pl.ds(0, 16)], sem("p0"))
        wait(qj.at[0], sem("q10"))
        wait(r1s.at[0], sem("r10"))

    wait(pj.at[:, pl.ds(0, 64)], sem("pa"))
    wait(pj.at[:, pl.ds(0, 48)], sem("pb"))
    wait(pj.at[:, pl.ds(0, 128)], sem("ps"))
    wait(gb.at[pl.ds(0, 4)], sem("ga"))
    wait(gb.at[pl.ds(0, 3)], sem("gb"))
    wait(fa.at[pl.ds(0, 31)], sem("fa"))
    wait(st.at[pl.ds(0, 15)], sem("st"))
    wait(oqs.at[pl.ds(0, 15)], sem("oq"))
    wait(ops.at[pl.ds(0, 15)], sem("op"))
    wait(fo.at[pl.ds(0, 31)], sem("fo"))
    for h in range(2):
        wait(outr.at[h], sem("rout", h))
        for i in range(4):
            out_ref[1 - b, place(h * 4 + i)] = outr[h, i * 64 : i * 64 + 64].astype(F32)
        wait(outs.at[h], sem("out", h))


def local(
    query_out, query_in, passage_out, passage_in_sum, passage_len, positive, proj_in, proj_out, test_grads
):
    out = pl.pallas_call(
        kernel,
        name="attribution",
        out_shape=jax.ShapeDtypeStruct((2, 512, 256), F32),
        in_specs=[pl.BlockSpec(memory_space=pl.ANY)] * 9,
        out_specs=pl.BlockSpec(memory_space=pltpu.VMEM),
        scratch_shapes=[
            pltpu.VMEM((288, 256), BF16),
            pltpu.VMEM((224, 256), BF16),
            pltpu.VMEM((256, 224), BF16),
            pltpu.VMEM((224, 256), BF16),
            pltpu.VMEM((224, 256), BF16),
            pltpu.VMEM((1, 256), jnp.int32),
            pltpu.VMEM((1, 256), jnp.int32),
            pltpu.VMEM((64, 224), BF16),
            pltpu.VMEM((64, 224), BF16),
            pltpu.VMEM((16, 288, 256), BF16),
            pltpu.VMEM((16, 256, 224), BF16),
            pltpu.VMEM((8, 64, 4096), BF16),
            pltpu.VMEM((16, 16, 128), F32),
            pltpu.VMEM((16, 16, 128), F32),
            pltpu.VMEM((32, 16, 128), F32),
            pltpu.VMEM((32, 16, 128), F32),
            pltpu.VMEM((16, 2, 256), F32),
            pltpu.VMEM((16, 16, 64), F32),
            pltpu.VMEM((16, 16, 64), F32),
            pltpu.VMEM((16, 16, 64), F32),
            pltpu.VMEM((16, 16, 64), F32),
            pltpu.VMEM((1, 256), jnp.int32),
            pltpu.VMEM((2, 128, 256), F32),
            pltpu.VMEM((2, 128, 256), F32),
            pltpu.VMEM((2, 4096, 256), BF16),
            pltpu.VMEM((2, 256, 256), BF16),
            pltpu.VMEM((2, 256, 256), BF16),
            pltpu.SemaphoreType.DMA((NSEM,)),
        ],
        compiler_params=pltpu.CompilerParams(
            collective_id=0, has_side_effects=True, vmem_limit_bytes=62 * 1024 * 1024
        ),
    )(
        query_out.T,
        passage_out.T,
        query_in.T,
        passage_in_sum.T,
        passage_len[None, :],
        positive[None, :],
        proj_in.T,
        proj_out.T,
        test_grads,
    )
    return out.reshape(1024, 256).T


def solution(mesh):
    return jax.shard_map(
        local,
        mesh=mesh,
        in_specs=(
            P("train", "test"),
            P("train", "test"),
            P("train", "test"),
            P("train", "test"),
            P("train"),
            P("train"),
            P("test", None),
            P("test", None),
            P(("test", "train"), None),
        ),
        out_specs=P("train", "test"),
        check_vma=False,
    )
```

time: 96.7 us -> 79.5 us (0.82)
  Pallas kernels: 90.5 us -> 76.9 us
  local copies, waits for them, and re-layouts: 5.81 us -> 2.53 us
    pallas_call x1, Pallas kernels: 90.5 us -> 76.9 us  [local(): pl.pallas_call(kernel, name='attribution', out_shape=jax.ShapeDtypeStruct...]
    unnamed x17 -> x0, local copies, waits for them, and re-layouts: 4.5 us -> none
    reshape x1, local copies, waits for them, and re-layouts: 1.31 us -> 2.53 us  [local(): return out.reshape(1024, 256).T]
where the time goes in v2:
time: 79.5 us; the launch traced here: 79.4 us
  Pallas kernels  76.9 us (97%)
  local copies, waits for them, and re-layouts  2.53 us (3%)
    pallas_call x1, Pallas kernels, local(): pl.pallas_call(kernel, name='attribution', out_shape=jax.ShapeDtypeStruct...  76.9 us
    reshape x1, local copies, waits for them, and re-layouts, local(): return out.reshape(1024, 256).T  2.53 us

profile of v2, /device:TPU:1, one launch (start us, length us, event | category | flops | bytes accessed | tf_op | source)
XLA Modules:
  0.0 79.4 jit_solution(15427499423875084332)
XLA Ops:
  0.0 76.9 %attribution.1 = f32[2,512,256]{2,1,0:T(8,128)} custom-call(bf16[224,256]{1,0:T(8,128)(2,1)} %bitcast.11, bf16[224,256]{1,0:T(8,128)(2,1)} %bitcast.12, bf16[224,256]{1,0:T(8,128)(2,1)} %bitcast.13, bf16[224,256]{1,0:T(8,128)(2,1)} %bitcast.14, s32[1,256]{1,0:T(1,128)} %bitcast.17, s32[1,256]{1,0:T(1,128)} %bitcast.18, bf16[64,224]{1,0:T(8,128)(2,1)} %bitcast.15, ...), custom_call_target="tpu_custom_call" | custom-call | tf_op jit(solution)/shard_map/attribution/pallas_call | solution.py:450
  76.9 2.5 %copy.10 = f32[1024,256]{0,1:T(8,128)} copy(f32[1024,256]{1,0:T(8,128)} %bitcast.10) | data formatting | bytes 2097152 | tf_op jit(solution)/shard_map/reshape | solution.py:500
